TPU v7x, 256 devices: a whole 4x4x8 slice. The times are simulated.
256 devices in a mesh: dp: 32 (over x, z), block: 8 (over y, core).
Axes of the slice: x: 4, y: 4, z: 8, core: 2. Of those that a mesh axis runs over, the one named last changes fastest.
Arguments:
- tokens: bfloat16 [32, 256, 4096], P('dp', 'block'), may hold values from -6 to 6
- cotangent: bfloat16 [32, 256, 4096], P('dp', 'block'), may hold values from -6 to 6
- w_up: bfloat16 [8, 4096, 512], P('block'), may hold values from -0.09375 to 0.09375
- w_down: bfloat16 [8, 512, 4096], P('block'), may hold values from -0.25 to 0.25
- active: int32 [32, 8], replicated, may hold values from 0 to 1, as said below
- width: int32 [32], replicated, may hold values from 8 to 16
- counts: int32 [8], replicated, may hold values from 32 to 127
Outputs:
- mixed: bfloat16 [32, 256, 4096], P('dp', 'block')
- input_grad: bfloat16 [32, 256, 4096], P('dp', 'block')
- up_grad: float32 [8, 4096, 512], P('block', 'dp')
- down_grad: float32 [8, 512, 4096], P('block', None, 'dp')
Inputs may be any that keep to these rules, and one draw needn't show every extreme that they name: `active`: 0 or 1; blocks differ in how many micro-batches use them. micro-batch i uses the first 256 * width[i] features.
All inputs are finite; a program needn't handle non-finite values.
Results may differ from a plain program's by a relative error of at most 0.019.
Values may be sent and summed in bfloat16 or wider, within the bound.
No kernel may reach another device: no remote copies, remote signals or barrier semaphores. Data moves between devices by JAX's collectives and lax.ppermute only.
A program may use at most 128 MiB of HBM per device.

v0:
```python
import math
import jax
import jax.numpy as jnp
from jax import lax
from jax.sharding import PartitionSpec as P

GELU_C = math.sqrt(2.0 / math.pi)


def gelu_parts(pre_vals):
    tanh_val = jnp.tanh(GELU_C * (pre_vals + 0.044715 * pre_vals * pre_vals * pre_vals))
    gelu_value = 0.5 * pre_vals * (1.0 + tanh_val)
    gelu_slope = 0.5 * (1.0 + tanh_val) + 0.5 * pre_vals * (1.0 - tanh_val * tanh_val) * GELU_C * (
        1.0 + 3.0 * 0.044715 * pre_vals * pre_vals
    )
    return (gelu_value, gelu_slope)


def local(tokens, cotangent, w_up, w_down, active, width, counts):
    micro_index = lax.axis_index("dp")
    owner_index = lax.axis_index("block")
    local_count = w_up.shape[0]
    feats = tokens.shape[2]
    start_block = owner_index * local_count
    act_row = lax.dynamic_slice(active, (micro_index, start_block), (1, local_count))[0]
    gate_row = act_row.astype(jnp.float32)
    counts_here = lax.dynamic_slice(counts, (start_block,), (local_count,)).astype(jnp.float32)
    scale_row = gate_row / counts_here
    width_step = lax.dynamic_slice(width, (micro_index,), (1,))[0]
    width_limit = feats // 16 * width_step
    feat_mask = (lax.iota(jnp.int32, feats) < width_limit).astype(jnp.bfloat16)
    gathered = (
        lax.all_gather(tokens, "block", axis=1, tiled=True),
        lax.all_gather(cotangent, "block", axis=1, tiled=True),
    )
    whole_x = gathered[0][0]
    whole_dy = gathered[1][0]
    masked_x = whole_x * feat_mask
    masked_dy = whole_dy * feat_mask
    pre_act = jnp.einsum("rd,bdu->bru", masked_x, w_up, preferred_element_type=jnp.float32)
    gelu_value, gelu_slope = gelu_parts(pre_act)
    hidden = gelu_value.astype(jnp.bfloat16)
    products = jnp.einsum("bru,bud->brd", hidden, w_down, preferred_element_type=jnp.float32)
    mixed_sum = lax.psum_scatter(
        jnp.sum(products * gate_row[:, None, None], axis=0).astype(jnp.bfloat16),
        "block",
        scatter_dimension=0,
        tiled=True,
    ).astype(jnp.float32)
    down_term = scale_row[:, None, None] * jnp.einsum(
        "bru,rd->bud", hidden, masked_dy, preferred_element_type=jnp.float32
    )
    back_proj = jnp.einsum("rd,bud->bru", masked_dy, w_down, preferred_element_type=jnp.float32)
    grad_hidden = (back_proj * gelu_slope).astype(jnp.bfloat16)
    up_term = scale_row[:, None, None] * jnp.einsum(
        "rd,bru->bdu", masked_x, grad_hidden, preferred_element_type=jnp.float32
    )
    up_grad, down_grad = (
        lax.psum_scatter(
            up_term.astype(jnp.bfloat16), "dp", scatter_dimension=1, tiled=True
        ).astype(jnp.float32),
        lax.psum_scatter(
            down_term.astype(jnp.bfloat16), "dp", scatter_dimension=2, tiled=True
        ).astype(jnp.float32),
    )
    products = jnp.einsum("bru,bdu->brd", grad_hidden, w_up, preferred_element_type=jnp.float32)
    input_sum = lax.psum_scatter(
        jnp.sum(products * gate_row[:, None, None], axis=0).astype(jnp.bfloat16),
        "block",
        scatter_dimension=0,
        tiled=True,
    ).astype(jnp.float32)
    mask_float = feat_mask.astype(jnp.float32)
    mixed = (tokens[0].astype(jnp.float32) + mask_float * mixed_sum).astype(jnp.bfloat16)[None]
    input_grad = (cotangent[0].astype(jnp.float32) + mask_float * input_sum).astype(jnp.bfloat16)[
        None
    ]
    return (mixed, input_grad, up_grad, down_grad)


def solution(mesh):
    in_specs = (
        P("dp", "block", None),
        P("dp", "block", None),
        P("block", None, None),
        P("block", None, None),
        P(),
        P(),
        P(),
    )
    out_specs = (
        P("dp", "block", None),
        P("dp", "block", None),
        P("block", "dp", None),
        P("block", None, "dp"),
    )
    return jax.shard_map(local, mesh=mesh, in_specs=in_specs, out_specs=out_specs, check_vma=False)
```

profile of v0, /device:TPU:8, one launch (start us, length us, event | category | flops | bytes accessed | tf_op | source)
XLA Modules:
  0.0 608.2 jit_solution(4567592196904731173)
XLA Ops:
  7.2 0.0 all-gather.3.cloned.1.call-start
  7.2 0.7 all-gather.3.cloned.1.call-update
  7.9 0.0 all-gather.5.cloned.1.call-start
  7.9 0.7 all-gather.5.cloned.1.call-update
  8.6 0.0 reduce-scatter.11.cloned.1.call-start
  8.7 1.2 dynamic_slice.9
  9.9 1.3 dynamic_slice.10
  12.5 27.0 %all-gather.3.cloned.1.call-done = bf16[1,256,4096]{2,1,0:T(8,128)(2,1)} async-done(((bf16[1,32,4096]{2,1,0:T(8,128)(2,1)}), bf16[1,256,4096]{2,1,0:T(8,128)(2,1)}) %all-gather.3.cloned.1.call-update) | async-done | bytes 2097168 | tf_op jit(solution)/shard_map/all_gather | solution.py:33
  39.6 4.1 fusion.18
  43.6 25.9 %all-gather.5.cloned.1.call-done = bf16[1,256,4096]{2,1,0:T(8,128)(2,1)} async-done(((bf16[1,32,4096]{2,1,0:T(8,128)(2,1)}), bf16[1,256,4096]{2,1,0:T(8,128)(2,1)}) %all-gather.5.cloned.1.call-update) | async-done | bytes 2097168 | tf_op jit(solution)/shard_map/all_gather | solution.py:34
  69.5 0.0 copy-start.3
  69.5 4.4 fusion.38
  73.9 0.0 copy-done.3
  74.0 2.7 fusion.3
  76.7 0.0 reduce-scatter.11.cloned.1.call-update
  76.7 0.0 copy-start.5
  76.7 0.0 copy-start
  76.7 0.0 reduce-scatter.9.cloned.1.call-start
  76.8 5.0 fusion.2
  81.7 0.0 reduce-scatter.9.cloned.1.call-update
  81.8 0.0 reduce-scatter.13.cloned.1.call-start
  81.8 0.0 copy-done.5
  81.8 0.6 dynamic_slice.11
  83.1 0.0 copy-done
  83.1 3.3 fusion
  86.4 19.0 %copy.13 = bf16[1,4096,512]{2,0,1:T(2,128)(2,1)} copy(bf16[1,4096,512]{1,2,0:T(8,128)(2,1)} %fusion) | data formatting | bytes 8388608
  105.3 6.7 %copy.22 = bf16[4096,1,512]{2,0,1:T(8,128)(2,1)} copy(bf16[4096,1,512]{2,1,0:T(2,128)(2,1)} %bitcast.100) | data formatting | bytes 8388608
  112.0 0.0 reduce-scatter.13.cloned.1.call-update
  112.0 0.0 reduce-scatter.15.cloned.1.call-start
  112.1 1.5 copy-done.4
  113.6 3.3 fusion.1
  116.9 18.9 %copy.15 = bf16[1,512,4096]{1,0,2:T(2,128)(2,1)} copy(bf16[1,512,4096]{2,1,0:T(8,128)(2,1)} %fusion.1) | data formatting | bytes 8388608
  135.9 6.6 %copy.21 = bf16[4096,1,512]{2,0,1:T(8,128)(2,1)} copy(bf16[4096,1,512]{2,1,0:T(2,128)(2,1)} %bitcast.101) | data formatting | bytes 8388608
  142.5 0.0 copy-start.2
  142.5 0.0 reduce-scatter.15.cloned.1.call-update
  142.5 0.0 reduce-scatter.11.cloned.1.call-done
  142.6 5.8 reduce-scatter.9.cloned.1.call-done
  148.4 0.0 copy-done.1
  148.4 0.0 copy-done.2
  148.4 2.0 fusion.55
  150.4 225.3 %reduce-scatter.13.cloned.1.call-done = bf16[128,512]{1,0:T(8,128)(2,1)} async-done(((bf16[4096,512]{1,0:T(8,128)(2,1)}), bf16[128,512]{1,0:T(8,128)(2,1)}) %reduce-scatter.13.cloned.1.call-update) | async-done | bytes 131088
  375.7 1.0 reshape_bitcast_fusion.1
  376.7 0.2 copy.14
  376.9 0.8 copy.12
  377.7 221.6 %reduce-scatter.15.cloned.1.call-done = bf16[128,512]{1,0:T(8,128)(2,1)} async-done(((bf16[4096,512]{1,0:T(8,128)(2,1)}), bf16[128,512]{1,0:T(8,128)(2,1)}) %reduce-scatter.15.cloned.1.call-update) | async-done | bytes 131088
  599.4 1.0 reshape_bitcast_fusion
  600.4 0.2 copy.16
  600.6 0.7 convert_element_type.106
  (4 shorter events, 0.0 us)
Async XLA Ops:
  7.2 32.4 %all-gather.3.cloned.1.call-start = ((), (), s32[]{:S(2)}) async-start(), calls=%async_computation.4 | async-start | bytes 2359296 | tf_op jit(solution)/shard_map/all_gather | solution.py:33
  7.9 61.6 %all-gather.5.cloned.1.call-start = ((), (), s32[]{:S(2)}) async-start(), calls=%async_computation.6 | async-start | bytes 2359296 | tf_op jit(solution)/shard_map/all_gather | solution.py:34
  8.6 133.9 %reduce-scatter.11.cloned.1.call-start = ((), (), s32[]{:S(2)}) async-start(), calls=%async_computation.7 | async-start | bytes 2359296 | tf_op jit(solution)/shard_map/reduce_scatter | solution.py:67
  69.5 4.4 copy-start.3
  76.7 5.1 copy-start.5
  76.7 6.4 %copy-start = (bf16[1,256,4096]{2,1,0:T(8,128)(2,1)S(1)}, bf16[1,256,4096]{2,1,0:T(8,128)(2,1)}, u32[]{:S(2)}) copy-start(bf16[1,256,4096]{2,1,0:T(8,128)(2,1)} %all-gather.3.cloned.1.call-done) | copy-start | bytes 6291460
  76.7 71.7 %reduce-scatter.9.cloned.1.call-start = ((), (), s32[]{:S(2)}) async-start(), calls=%async_computation.5 | async-start | bytes 2359296 | tf_op jit(solution)/shard_map/reduce_scatter | solution.py:44
  81.8 293.9 %reduce-scatter.13.cloned.1.call-start = ((), (), s32[]{:S(2)}) async-start(), calls=%async_computation.8 | async-start | bytes 4325376
  112.0 1.6 copy-start.4
  112.0 487.3 %reduce-scatter.15.cloned.1.call-start = ((), (), s32[]{:S(2)}) async-start(), calls=%async_computation.9 | async-start | bytes 4325376
  142.5 5.9 copy-start.1
  142.5 5.9 copy-start.2
Sparse Core Ops, SparseCore 0:
  9.9 29.6 all-gather.2
  41.4 28.0 all-gather.4
  76.8 34.1 reduce-scatter.10
  113.4 34.9 reduce-scatter.8
  152.2 223.4 reduce-scatter.12
  379.9 219.3 reduce-scatter.14
where the time goes:
time: 610 us; the launch traced here: 608 us
  waiting for transfers between devices  507 us (83%)
  local copies, waits for them, and re-layouts  59.1 us (10%)
  matrix products  22.8 us (4%)
  between operations  16.2 us (3%)
    unnamed x8, waiting for transfers between devices  448 us
    unnamed x21, local copies, waits for them, and re-layouts  56 us
    all_gather x1, waiting for transfers between devices, local(): lax.all_gather(tokens, 'block', axis=1, tiled=True)  27 us
    all_gather x1, waiting for transfers between devices, local(): lax.all_gather(cotangent, 'block', axis=1, tiled=True)  25.9 us
  transfers between devices with their start and end apart: 6, of which 5 were waited for; matrix products, arithmetic and copies ran while one was open for 12% of the time, Pallas kernels for 0%

commit v1 on v0

--- a/solution.py
+++ b/solution.py
@@ -5,6 +5,22 @@
 from jax.sharding import PartitionSpec as P
 
 GELU_C = math.sqrt(2.0 / math.pi)
+
+
+def collect(x, axis, dim):
+    ways, here, turn = (lax.axis_size(axis), lax.axis_index(axis), x.shape[dim])
+    shape = [n * ways if d == dim else n for d, n in enumerate(x.shape)]
+    full = lax.dynamic_update_slice_in_dim(jnp.zeros(shape, x.dtype), x, here * turn, axis=dim)
+    going_up = going_down = x
+    for far in range(1, ways // 2 + 1):
+        going_up = lax.ppermute(going_up, axis, [(d, (d + 1) % ways) for d in range(ways)])
+        full = lax.dynamic_update_slice_in_dim(full, going_up, (here - far) % ways * turn, axis=dim)
+        if 2 * far < ways:
+            going_down = lax.ppermute(going_down, axis, [(d, (d - 1) % ways) for d in range(ways)])
+            full = lax.dynamic_update_slice_in_dim(
+                full, going_down, (here + far) % ways * turn, axis=dim
+            )
+    return full
 
 
 def gelu_parts(pre_vals):
@@ -29,10 +45,7 @@
     width_step = lax.dynamic_slice(width, (micro_index,), (1,))[0]
     width_limit = feats // 16 * width_step
     feat_mask = (lax.iota(jnp.int32, feats) < width_limit).astype(jnp.bfloat16)
-    gathered = (
-        lax.all_gather(tokens, "block", axis=1, tiled=True),
-        lax.all_gather(cotangent, "block", axis=1, tiled=True),
-    )
+    gathered = (lax.all_gather(tokens, "block", axis=1, tiled=True), collect(cotangent, "block", 1))
     whole_x = gathered[0][0]
     whole_dy = gathered[1][0]
     masked_x = whole_x * feat_mask

time: 610 us -> 583 us (0.956)
  waiting for transfers between devices: 507 us -> 476 us
    all_gather x1 -> x0, waiting for transfers between devices: 25.9 us -> none  [local(): lax.all_gather(cotangent, 'block', axis=1, tiled=True)]
    all_gather x1, waiting for transfers between devices: 27 us -> 8.31 us  [local(): lax.all_gather(tokens, 'block', axis=1, tiled=True)]
    ppermute x0 -> x7, waiting for transfers between devices: none -> 15 us  [the longest x4 14.5 us: collect(): lax.ppermute(going_up, axis, [(d, (d + 1) % ways) for d in range(ways)])]
    unnamed x8 -> x7, waiting for transfers between devices: 448 us -> 447 us
  transfers between devices with their start and end apart: 6 -> 12, of which waited for: 5 -> 10; matrix products, arithmetic and copies ran while one was open for 12% -> 12% of each run, Pallas kernels for 0% -> 0%
where the time goes in v1:
time: 583 us; the launch traced here: 581 us
  waiting for transfers between devices  476 us (82%)
  local copies, waits for them, and re-layouts  58.4 us (10%)
  matrix products  21.5 us (4%)
  between operations  16.1 us (3%)
  starting transfers between devices  6.2 us (1%)
    unnamed x7, waiting for transfers between devices  447 us
    unnamed x21, local copies, waits for them, and re-layouts  55.6 us
    ppermute x4, waiting for transfers between devices, collect(): lax.ppermute(going_up, axis, [(d, (d + 1) % ways) for d in range(ways)])  14.5 us
  transfers between devices with their start and end apart: 12, of which 10 were waited for; matrix products, arithmetic and copies ran while one was open for 12% of the time, Pallas kernels for 0%

profile of v1, /device:TPU:8, one launch (start us, length us, event | category | flops | bytes accessed | tf_op | source)
XLA Modules:
  0.0 581.0 jit_solution(7159584044104785682)
XLA Ops:
  7.2 0.0 all-gather.2.cloned.1.call-start
  7.2 0.0 collective-permute-start
  7.3 1.7 collective-permute-start.1
  9.0 0.0 all-gather.2.cloned.1.call-update
  9.0 0.0 reduce-scatter.11.cloned.1.call-start
  9.1 0.2 squeeze.25
  9.5 0.6 dynamic_slice.9
  10.1 1.3 dynamic_slice.10
  12.7 0.6 collective-permute-done
  13.3 2.0 collective-permute-start.3
  15.3 3.7 collective-permute-done.2
  19.1 0.1 collective-permute-done.3
  19.2 2.2 collective-permute-start.5
  21.4 3.4 collective-permute-done.4
  24.9 0.4 collective-permute-done.5
  25.3 6.8 %collective-permute-done.6 = bf16[1,32,4096]{2,1,0:T(8,128)(2,1)S(1)} collective-permute-done((bf16[1,32,4096]{2,1,0:T(8,128)(2,1)S(1)}, bf16[1,32,4096]{2,1,0:T(8,128)(2,1)S(1)}, u32[]{:S(2)}, u32[]{:S(2)}) %collective-permute-start.6) | collective-permute-done | bytes 262176 | tf_op jit(solution)/shard_map/ppermute | solution.py:16
  32.1 8.3 %all-gather.2.cloned.1.call-done = bf16[1,256,4096]{2,1,0:T(8,128)(2,1)} async-done(((bf16[1,32,4096]{2,1,0:T(8,128)(2,1)}), bf16[1,256,4096]{2,1,0:T(8,128)(2,1)}) %all-gather.2.cloned.1.call-update) | async-done | bytes 2097168 | tf_op jit(solution)/shard_map/all_gather | solution.py:48
  40.5 4.2 fusion.16
  44.7 1.6 fusion.36
  46.3 0.6 copy-done.2
  46.9 2.7 fusion.3
  49.6 0.0 reduce-scatter.11.cloned.1.call-update
  49.6 0.0 reduce-scatter.9.cloned.1.call-start
  49.7 4.8 fusion.2
  54.5 0.0 reduce-scatter.9.cloned.1.call-update
  54.5 0.0 reduce-scatter.13.cloned.1.call-start
  54.6 0.6 copy-done.5
  55.2 0.6 dynamic_slice.11
  56.4 4.8 fusion
  61.3 18.9 %copy.13 = bf16[1,4096,512]{2,0,1:T(2,128)(2,1)} copy(bf16[1,4096,512]{1,2,0:T(8,128)(2,1)} %fusion) | data formatting | bytes 8388608
  80.2 6.6 %copy.22 = bf16[4096,1,512]{2,0,1:T(8,128)(2,1)} copy(bf16[4096,1,512]{2,1,0:T(2,128)(2,1)} %bitcast.101) | data formatting | bytes 8388608
  86.8 0.0 reduce-scatter.13.cloned.1.call-update
  86.8 0.0 reduce-scatter.15.cloned.1.call-start
  86.9 3.3 fusion.1
  90.2 18.9 %copy.15 = bf16[1,512,4096]{1,0,2:T(2,128)(2,1)} copy(bf16[1,512,4096]{2,1,0:T(8,128)(2,1)} %fusion.1) | data formatting | bytes 8388608
  109.2 6.6 %copy.21 = bf16[4096,1,512]{2,0,1:T(8,128)(2,1)} copy(bf16[4096,1,512]{2,1,0:T(2,128)(2,1)} %bitcast.102) | data formatting | bytes 8388608
  115.8 0.0 reduce-scatter.15.cloned.1.call-update
  115.8 0.0 reduce-scatter.11.cloned.1.call-done
  115.9 6.0 %reduce-scatter.9.cloned.1.call-done = bf16[32,4096]{1,0:T(8,128)(2,1)} async-done(((bf16[256,4096]{1,0:T(8,128)(2,1)}), bf16[32,4096]{1,0:T(8,128)(2,1)}) %reduce-scatter.9.cloned.1.call-update) | async-done | bytes 262160 | tf_op jit(solution)/shard_map/reduce_scatter | solution.py:57
  121.8 2.0 fusion.51
  123.8 225.0 %reduce-scatter.13.cloned.1.call-done = bf16[128,512]{1,0:T(8,128)(2,1)} async-done(((bf16[4096,512]{1,0:T(8,128)(2,1)}), bf16[128,512]{1,0:T(8,128)(2,1)}) %reduce-scatter.13.cloned.1.call-update) | async-done | bytes 131088
  348.8 1.0 reshape_bitcast_fusion.1
  349.9 0.2 copy.14
  350.1 0.8 copy.12
  350.9 221.6 %reduce-scatter.15.cloned.1.call-done = bf16[128,512]{1,0:T(8,128)(2,1)} async-done(((bf16[4096,512]{1,0:T(8,128)(2,1)}), bf16[128,512]{1,0:T(8,128)(2,1)}) %reduce-scatter.15.cloned.1.call-update) | async-done | bytes 131088
  572.5 1.0 reshape_bitcast_fusion
  573.6 0.2 copy.16
  573.7 0.7 convert_element_type.102
  (24 shorter events, 0.2 us)
Async XLA Ops:
  7.2 2.1 copy-start
  7.2 2.3 copy-start.4
  7.2 33.3 %all-gather.2.cloned.1.call-start = ((), (), s32[]{:S(2)}) async-start(), calls=%async_computation.4 | async-start | bytes 2359296 | tf_op jit(solution)/shard_map/all_gather | solution.py:48
  7.2 6.0 %collective-permute-start = (bf16[1,32,4096]{2,1,0:T(8,128)(2,1)}, bf16[1,32,4096]{2,1,0:T(8,128)(2,1)S(1)}, u32[]{:S(2)}, u32[]{:S(2)}) collective-permute-start(bf16[1,32,4096]{2,1,0:T(8,128)(2,1)} %param.8), channel_id=1, source_target_pairs={{0,1},{1,2},{2,3},{3,4},{4,5},{5,6},{6,7},{7,0},{8,9},{9,10},{10,1... | collective-permute-start | bytes 786440 | tf_op jit(solution)/shard_map/ppermute | solution.py:16
  7.3 6.0 %collective-permute-start.1 = (bf16[1,32,4096]{2,1,0:T(8,128)(2,1)}, bf16[1,32,4096]{2,1,0:T(8,128)(2,1)S(1)}, u32[]{:S(2)}, u32[]{:S(2)}) collective-permute-start(bf16[1,32,4096]{2,1,0:T(8,128)(2,1)} %param.8), channel_id=1, source_target_pairs={{0,7},{1,0},{2,1},{3,2},{4,3},{5,4},{6,5},{7,6},{8,15},{9,8},{10,9... | collective-permute-start | bytes 786440 | tf_op jit(solution)/shard_map/ppermute | solution.py:19
  9.0 106.8 %reduce-scatter.11.cloned.1.call-start = ((), (), s32[]{:S(2)}) async-start(), calls=%async_computation.6 | async-start | bytes 2359296 | tf_op jit(solution)/shard_map/reduce_scatter | solution.py:80
  13.3 5.8 collective-permute-start.2
  13.3 5.9 %collective-permute-start.3 = (bf16[1,32,4096]{2,1,0:T(8,128)(2,1)S(1)}, bf16[1,32,4096]{2,1,0:T(8,128)(2,1)S(1)}, u32[]{:S(2)}, u32[]{:S(2)}) collective-permute-start(bf16[1,32,4096]{2,1,0:T(8,128)(2,1)S(1)} %collective-permute-done.1), channel_id=1, source_target_pairs={{0,7},{1,0},{2,1},{3,2},{4,3},{5,4},{6,5},{7,6},{8,15},{9,8},{10,9... | collective-permute-start | bytes 786440 | tf_op jit(solution)/shard_map/ppermute | solution.py:19
  19.0 5.8 collective-permute-start.4
  19.2 6.1 %collective-permute-start.5 = (bf16[1,32,4096]{2,1,0:T(8,128)(2,1)S(1)}, bf16[1,32,4096]{2,1,0:T(8,128)(2,1)S(1)}, u32[]{:S(2)}, u32[]{:S(2)}) collective-permute-start(bf16[1,32,4096]{2,1,0:T(8,128)(2,1)S(1)} %collective-permute-done.3), channel_id=1, source_target_pairs={{0,7},{1,0},{2,1},{3,2},{4,3},{5,4},{6,5},{7,6},{8,15},{9,8},{10,9... | collective-permute-start | bytes 786440 | tf_op jit(solution)/shard_map/ppermute | solution.py:19
  24.8 7.3 %collective-permute-start.6 = (bf16[1,32,4096]{2,1,0:T(8,128)(2,1)S(1)}, bf16[1,32,4096]{2,1,0:T(8,128)(2,1)S(1)}, u32[]{:S(2)}, u32[]{:S(2)}) collective-permute-start(bf16[1,32,4096]{2,1,0:T(8,128)(2,1)S(1)} %collective-permute-done.4), channel_id=1, source_target_pairs={{0,1},{1,2},{2,3},{3,4},{4,5},{5,6},{6,7},{7,0},{8,9},{9,10},{10,1... | collective-permute-start | bytes 786440 | tf_op jit(solution)/shard_map/ppermute | solution.py:16
  40.5 4.2 copy-start.3
  44.7 2.2 copy-start.2
  49.6 72.2 %reduce-scatter.9.cloned.1.call-start = ((), (), s32[]{:S(2)}) async-start(), calls=%async_computation.5 | async-start | bytes 2359296 | tf_op jit(solution)/shard_map/reduce_scatter | solution.py:57
  54.5 0.7 copy-start.5
  54.5 294.3 %reduce-scatter.13.cloned.1.call-start = ((), (), s32[]{:S(2)}) async-start(), calls=%async_computation.7 | async-start | bytes 4325376
  86.8 485.7 %reduce-scatter.15.cloned.1.call-start = ((), (), s32[]{:S(2)}) async-start(), calls=%async_computation.8 | async-start | bytes 4325376
  115.8 6.0 %copy-start.1 = (bf16[1,32,4096]{2,1,0:T(8,128)(2,1)S(1)}, bf16[1,32,4096]{2,1,0:T(8,128)(2,1)}, u32[]{:S(2)}) copy-start(bf16[1,32,4096]{2,1,0:T(8,128)(2,1)} %param.7) | copy-start | bytes 786436
Sparse Core Ops, SparseCore 0:
  9.9 30.5 all-gather.1
  49.7 34.4 reduce-scatter.10
  86.8 35.0 reduce-scatter.8
  125.6 223.1 reduce-scatter.12
  353.1 219.3 reduce-scatter.14
